TPU v7x, 32 devices: a whole 2x2x4 slice. The times are simulated.
32 devices in a mesh: fsdp: 8 (over z, y), seq: 4 (over x, core).
Axes of the slice: x: 2, y: 2, z: 4, core: 2. Of those that a mesh axis runs over, the one named last changes fastest.
Arguments:
- layer_input: bfloat16 [4096, 2048], P(('fsdp', 'seq')), may hold values from -6 to 6
- segment_ids: int32 [8, 512], P('fsdp'), may hold values from 0 to 7, as said below
- positions: int32 [4096], P('fsdp'), may hold values from 0 to 766, as said below
- ln1_gain: bfloat16 [2048], P(('fsdp', 'seq')), may hold values from 0.5 to 1.5
- ln1_bias: bfloat16 [2048], P(('fsdp', 'seq')), may hold values from -4 to 4
- qkv_weight: bfloat16 [2048, 6144], P(('fsdp', 'seq')), may hold values from -0.125 to 0.125
- qkv_bias: bfloat16 [6144], P(('fsdp', 'seq')), may hold values from -6 to 6
- out_weight: bfloat16 [2048, 2048], P(('fsdp', 'seq')), may hold values from -0.75 to 0.75
- ln2_gain: bfloat16 [2048], P(('fsdp', 'seq')), may hold values from 0.5 to 1.5
- ln2_bias: bfloat16 [2048], P(('fsdp', 'seq')), may hold values from -4 to 4
- gate_weight: bfloat16 [2048, 5632], P(('fsdp', 'seq')), may hold values from -0.125 to 0.125
- up_weight: bfloat16 [2048, 5632], P(('fsdp', 'seq')), may hold values from -0.125 to 0.125
- down_weight: bfloat16 [2048, 5632], P(('fsdp', 'seq')), may hold values from -0.078125 to 0.078125
- cotangent: bfloat16 [4096, 2048], P(('fsdp', 'seq')), may hold values from -6 to 6
Outputs:
- layer_output: bfloat16 [4096, 2048], P(('fsdp', 'seq'))
- input_grad: float32 [4096, 2048], P(('fsdp', 'seq'))
- ln1_gain_grad: float32 [2048], P(('fsdp', 'seq'))
- ln1_bias_grad: float32 [2048], P(('fsdp', 'seq'))
- qkv_weight_grad: float32 [2048, 6144], P(('fsdp', 'seq'))
- qkv_bias_grad: float32 [6144], P(('fsdp', 'seq'))
- out_weight_grad: float32 [2048, 2048], P(('fsdp', 'seq'))
- ln2_gain_grad: float32 [2048], P(('fsdp', 'seq'))
- ln2_bias_grad: float32 [2048], P(('fsdp', 'seq'))
- gate_weight_grad: float32 [2048, 5632], P(('fsdp', 'seq'))
- up_weight_grad: float32 [2048, 5632], P(('fsdp', 'seq'))
- down_weight_grad: float32 [2048, 5632], P(('fsdp', 'seq'))
Inputs may be any that keep to these rules, and one draw needn't show every extreme that they name: `segment_ids`: segment ids never fall along a sequence; each document holds 64 to 256 tokens, the first and last of a sequence may be cut. `positions`: A token's position counts from its document's first token, which for a sequence's first document may lie up to 511 tokens before the sequence.
All inputs are finite; a program needn't handle non-finite values.
Results may differ from a plain program's by a relative error of at most 0.012.
Values may be sent and summed in bfloat16 or wider, within the bound.
No kernel may reach another device: no remote copies, remote signals or barrier semaphores. Data moves between devices by JAX's collectives and lax.ppermute only.
A program may use at most 256 MiB of HBM per device.

v0:
```python
import jax
import jax.numpy as jnp
from jax import lax
from jax.sharding import PartitionSpec as P

HEADS = 32
HEAD_DIM = 64


def layer_norm(values, gain, shift):
    center = jnp.mean(values, axis=-1, keepdims=True)
    centered = values - center
    spread = jnp.mean(centered * centered, axis=-1, keepdims=True)
    return centered * lax.rsqrt(spread + 1e-05) * gain + shift


def rotary_tables(spots):
    inverse = 10000.0 ** (-jnp.arange(8).astype(jnp.float32) / 8.0)
    angle = spots.astype(jnp.float32)[:, None] * inverse[None, :]
    return (jnp.cos(angle), jnp.sin(angle))


def rotate(heads_view, cosine, sine):
    first = heads_view[..., :8]
    second = heads_view[..., 8:16]
    rest = heads_view[..., 16:]
    cos_part = cosine[:, None, :]
    sin_part = sine[:, None, :]
    return jnp.concatenate(
        [first * cos_part - second * sin_part, second * cos_part + first * sin_part, rest], axis=-1
    )


def contract_rows(left, right):
    return lax.dot_general(
        left, right, (((0,), (0,)), ((), ())), preferred_element_type=jnp.float32
    )


def contract_cols(left, right):
    return lax.dot_general(
        left, right, (((1,), (1,)), ((), ())), preferred_element_type=jnp.float32
    )


def swiglu(gate, up):
    return jax.nn.silu(gate) * up


def fetch_all(first, second, third, fourth, fifth):
    return (
        lax.all_gather(first, ("fsdp", "seq"), axis=0, tiled=True),
        lax.all_gather(second, ("fsdp", "seq"), axis=0, tiled=True),
        lax.all_gather(third, ("fsdp", "seq"), axis=0, tiled=True),
        lax.all_gather(fourth, ("fsdp", "seq"), axis=0, tiled=True),
        lax.all_gather(fifth, ("fsdp", "seq"), axis=0, tiled=True),
    )


def sum_all(first, second, third, fourth, fifth):
    return (
        lax.psum_scatter(first, ("fsdp", "seq"), scatter_dimension=0, tiled=True),
        lax.psum_scatter(second, ("fsdp", "seq"), scatter_dimension=0, tiled=True),
        lax.psum_scatter(third, ("fsdp", "seq"), scatter_dimension=0, tiled=True),
        lax.psum_scatter(fourth, ("fsdp", "seq"), scatter_dimension=0, tiled=True),
        lax.psum_scatter(fifth, ("fsdp", "seq"), scatter_dimension=0, tiled=True),
    )


def fetch_block(first, second):
    columns = (
        lax.all_to_all(first, "seq", split_axis=2, concat_axis=0, tiled=True),
        lax.all_to_all(second, "seq", split_axis=2, concat_axis=0, tiled=True),
    )
    return (
        lax.all_gather(columns[0], "fsdp", axis=0, tiled=True),
        lax.all_gather(columns[1], "fsdp", axis=0, tiled=True),
    )


def return_block(first, second):
    summed = (
        lax.psum_scatter(first, "fsdp", scatter_dimension=0, tiled=True),
        lax.psum_scatter(second, "fsdp", scatter_dimension=0, tiled=True),
    )
    return (
        lax.all_to_all(summed[0], "seq", split_axis=0, concat_axis=2, tiled=True),
        lax.all_to_all(summed[1], "seq", split_axis=0, concat_axis=2, tiled=True),
    )


def seq_rows(values):
    return lax.all_gather(values, "seq", axis=0, tiled=True)


def seq_sums(values):
    return lax.psum_scatter(values, "seq", scatter_dimension=0, tiled=True)


def split_heads(
    layer_input,
    segment_ids,
    positions,
    ln1_gain,
    ln1_bias,
    qkv_weight,
    qkv_bias,
    out_weight,
    ln2_gain,
    ln2_bias,
    gate_weight,
    up_weight,
    down_weight,
    cotangent,
):
    width = layer_input.shape[1]
    own_rows = qkv_weight.shape[0]
    hidden_units = gate_weight.shape[1]
    quarter = lax.axis_size("seq")
    seq_spot = lax.axis_index("seq")
    width_part = width // quarter
    units_part = hidden_units // quarter
    heads_here = HEADS // quarter
    small = fetch_all(qkv_bias, ln1_gain, ln1_bias, ln2_gain, ln2_bias)
    gain_one = small[1].astype(jnp.float32)
    shift_one = small[2].astype(jnp.float32)
    gain_two = small[3].astype(jnp.float32)
    shift_two = small[4].astype(jnp.float32)
    bias_here = (
        lax.dynamic_slice_in_dim(small[0].reshape(3, width), seq_spot * width_part, width_part, 1)
        .astype(jnp.float32)
        .reshape(3 * width_part)
    )

    def attn_blocks():
        return fetch_block(
            qkv_weight.reshape(own_rows, 3, width), out_weight.reshape(own_rows, 1, width)
        )

    def mlp_blocks():
        return fetch_block(
            jnp.stack([gate_weight, up_weight], axis=1),
            down_weight.reshape(own_rows, 1, hidden_units),
        )

    attn_fwd = attn_blocks()
    qkv_block = attn_fwd[0].reshape(width, 3 * width_part)
    out_block = attn_fwd[1].reshape(width, width_part)
    inputs = layer_input.astype(jnp.float32)
    normed_low = layer_norm(inputs, gain_one, shift_one).astype(jnp.bfloat16)
    normed_all = seq_rows(normed_low)
    length = normed_all.shape[0]
    mixed = jnp.dot(normed_all, qkv_block, preferred_element_type=jnp.float32) + bias_here
    cosine, sine = rotary_tables(positions)
    query_low = rotate(
        mixed[:, :width_part].reshape(length, heads_here, HEAD_DIM), cosine, sine
    ).astype(jnp.bfloat16)
    key_low = rotate(
        mixed[:, width_part : 2 * width_part].reshape(length, heads_here, HEAD_DIM), cosine, sine
    ).astype(jnp.bfloat16)
    value_low = (
        mixed[:, 2 * width_part :].reshape(length, heads_here, HEAD_DIM).astype(jnp.bfloat16)
    )
    segment_row = segment_ids[0]
    index = jnp.arange(length)

    def block_scores():
        scores = (
            jnp.einsum("thd,lhd->htl", query_low, key_low, preferred_element_type=jnp.float32)
            * 0.125
        )
        allowed = (segment_row[:, None] == segment_row[None, :]) & (
            index[None, :] <= index[:, None]
        )
        return jnp.where(allowed[None], scores, -1e30)

    scores = block_scores()
    top = jnp.max(scores, axis=-1, keepdims=True)
    expo = jnp.exp(scores - top)
    total = jnp.sum(expo, axis=-1, keepdims=True)
    probs = (expo / total).astype(jnp.bfloat16)
    log_sums = top + jnp.log(total)
    pieces = jnp.einsum("htl,lhd->thd", probs, value_low, preferred_element_type=jnp.float32)
    attended_low = pieces.reshape(length, width_part).astype(jnp.bfloat16)
    hidden = inputs + seq_sums(contract_cols(attended_low, out_block))
    mlp_fwd = mlp_blocks()
    pair_block = mlp_fwd[0].reshape(width, 2 * units_part)
    down_block = mlp_fwd[1].reshape(width, units_part)
    normed2_low = layer_norm(hidden, gain_two, shift_two).astype(jnp.bfloat16)
    normed2_all = seq_rows(normed2_low)
    gate_up = jnp.dot(normed2_all, pair_block, preferred_element_type=jnp.float32)
    gate = gate_up[:, :units_part]
    up = gate_up[:, units_part:]
    inner_low = swiglu(gate, up).astype(jnp.bfloat16)
    result = hidden + seq_sums(contract_cols(inner_low, down_block))
    mlp_back = mlp_blocks()
    pair_back = mlp_back[0].reshape(width, 2 * units_part)
    down_back = mlp_back[1].reshape(width, units_part)
    cotangent_all = seq_rows(cotangent)
    inner_grad = jnp.dot(cotangent_all, down_back, preferred_element_type=jnp.float32)
    down_grad = contract_rows(cotangent_all, inner_low)
    unused, pull_swiglu = jax.vjp(swiglu, gate, up)
    gate_grad, up_grad = pull_swiglu(inner_grad)
    pair_low = jnp.concatenate(
        [gate_grad.astype(jnp.bfloat16), up_grad.astype(jnp.bfloat16)], axis=1
    )
    pair_wgrad = contract_rows(normed2_all, pair_low)
    normed2_grad = seq_sums(contract_cols(pair_low, pair_back))
    unused_two, pull_norm_two = jax.vjp(layer_norm, hidden, gain_two, shift_two)
    hidden_part, gain_two_grad, shift_two_grad = pull_norm_two(normed2_grad)
    hidden_grad = cotangent.astype(jnp.float32) + hidden_part
    mlp_shares = return_block(
        pair_wgrad.reshape(width, 2, units_part), down_grad.reshape(width, 1, units_part)
    )
    attn_back = attn_blocks()
    qkv_back = attn_back[0].reshape(width, 3 * width_part)
    out_back = attn_back[1].reshape(width, width_part)
    branch_all = seq_rows(hidden_grad.astype(jnp.bfloat16))
    out_wgrad = contract_rows(branch_all, attended_low)
    attended_grad = (
        jnp.dot(branch_all, out_back, preferred_element_type=jnp.float32)
        .astype(jnp.bfloat16)
        .reshape(length, heads_here, HEAD_DIM)
    )
    scores = block_scores()
    probs = jnp.exp(scores - log_sums)
    probs_low = probs.astype(jnp.bfloat16)
    value_grad = jnp.einsum(
        "htl,thd->lhd", probs_low, attended_grad, preferred_element_type=jnp.float32
    )
    probs_grad = jnp.einsum(
        "thd,lhd->htl", attended_grad, value_low, preferred_element_type=jnp.float32
    )
    center = jnp.sum(probs * probs_grad, axis=-1, keepdims=True)
    scores_low = (probs * (probs_grad - center)).astype(jnp.bfloat16)
    query_pieces = (
        jnp.einsum("htl,lhd->thd", scores_low, key_low, preferred_element_type=jnp.float32) * 0.125
    )
    key_grad = (
        jnp.einsum("htl,thd->lhd", scores_low, query_low, preferred_element_type=jnp.float32)
        * 0.125
    )
    query_back = rotate(query_pieces, cosine, -sine).reshape(length, width_part)
    key_back = rotate(key_grad, cosine, -sine).reshape(length, width_part)
    mixed_low = jnp.concatenate(
        [query_back, key_back, value_grad.reshape(length, width_part)], axis=1
    ).astype(jnp.bfloat16)
    qkv_wgrad = contract_rows(normed_all, mixed_low)
    bias_part = jnp.sum(mixed_low.astype(jnp.float32), axis=0).reshape(3, width_part)
    slot_mask = (jnp.arange(quarter) == seq_spot).astype(jnp.float32)
    bias_whole = (bias_part[:, None, :] * slot_mask[None, :, None]).reshape(3 * width)
    normed_grad = seq_sums(contract_cols(mixed_low, qkv_back))
    unused_one, pull_norm_one = jax.vjp(layer_norm, inputs, gain_one, shift_one)
    input_part, gain_one_grad, shift_one_grad = pull_norm_one(normed_grad)
    input_grad = hidden_grad + input_part
    attn_shares = return_block(
        qkv_wgrad.reshape(width, 3, width_part), out_wgrad.reshape(width, 1, width_part)
    )
    small_shares = sum_all(bias_whole, gain_one_grad, shift_one_grad, gain_two_grad, shift_two_grad)
    gate_wgrad = mlp_shares[0][:, 0, :]
    up_wgrad = mlp_shares[0][:, 1, :]
    down_wgrad = mlp_shares[1].reshape(own_rows, hidden_units)
    qkv_share = attn_shares[0].reshape(own_rows, 3 * width)
    out_share = attn_shares[1].reshape(own_rows, width)
    return (
        result.astype(jnp.bfloat16),
        input_grad,
        small_shares[1],
        small_shares[2],
        qkv_share,
        small_shares[0],
        out_share,
        small_shares[3],
        small_shares[4],
        gate_wgrad,
        up_wgrad,
        down_wgrad,
    )


def body(
    layer_input,
    segment_ids,
    positions,
    ln1_gain,
    ln1_bias,
    qkv_weight,
    qkv_bias,
    out_weight,
    ln2_gain,
    ln2_bias,
    gate_weight,
    up_weight,
    down_weight,
    cotangent,
):
    return split_heads(
        layer_input,
        segment_ids,
        positions,
        ln1_gain,
        ln1_bias,
        qkv_weight,
        qkv_bias,
        out_weight,
        ln2_gain,
        ln2_bias,
        gate_weight,
        up_weight,
        down_weight,
        cotangent,
    )


def solution(mesh):
    placed = (
        P(("fsdp", "seq"), None),
        P("fsdp", None),
        P("fsdp"),
        P(("fsdp", "seq")),
        P(("fsdp", "seq")),
        P(("fsdp", "seq"), None),
        P(("fsdp", "seq")),
        P(("fsdp", "seq"), None),
        P(("fsdp", "seq")),
        P(("fsdp", "seq")),
        P(("fsdp", "seq"), None),
        P(("fsdp", "seq"), None),
        P(("fsdp", "seq"), None),
        P(("fsdp", "seq"), None),
    )
    return jax.shard_map(
        body,
        mesh=mesh,
        in_specs=placed,
        out_specs=(
            P(("fsdp", "seq"), None),
            P(("fsdp", "seq"), None),
            P(("fsdp", "seq")),
            P(("fsdp", "seq")),
            P(("fsdp", "seq"), None),
            P(("fsdp", "seq")),
            P(("fsdp", "seq"), None),
            P(("fsdp", "seq")),
            P(("fsdp", "seq")),
            P(("fsdp", "seq"), None),
            P(("fsdp", "seq"), None),
            P(("fsdp", "seq"), None),
        ),
        check_vma=False,
    )
```

profile of v0, /device:TPU:0, one launch (start us, length us, event | category | flops | bytes accessed | tf_op | source)
XLA Modules:
  0.0 2342.5 jit_solution(12369615966745718935)
XLA Ops:
  13.2 15.8 all_to_all.155
  35.5 43.4 %all-reduce.15 = (bf16[2048]{0:T(1024)(128)(2,1)S(1)}, bf16[2048]{0:T(1024)(128)(2,1)S(1)}, bf16[3,2048]{1,0:T(4,128)(2,1)S(1)}, bf16[2048]{0:T(1024)(128)(2,1)}, bf16[2048]{0:T(1024)(128)(2,1)}) all-reduce(bf16[2048]{0:T(1024)(128)(2,1)S(1)} %dynamic-update-slice.1, ...), channel_id=1, replica_groups=mesh['fsdp'=8,'seq'=4] {'fsdp','seq'}, use_global_device_ids=true, to_apply=%add.1 | all-reduce | flops 14336 | bytes 57344
  82.4 11.5 reduce
  106.9 28.3 %all-gather.11.cloned.1.call-done = bf16[2048,3,512]{2,0,1:T(8,128)(2,1)} async-done(((bf16[256,3,512]{2,0,1:T(8,128)(2,1)}), bf16[2048,3,512]{2,0,1:T(8,128)(2,1)}) %all-gather.11.cloned.1.call-update) | async-done | bytes 6291472 | tf_op jit(solution)/shard_map/all_gather | solution.py:76
  144.2 14.0 all-gather.9.cloned.1.call-done
  178.6 31.6 %all-gather.13.cloned.1.call-done = bf16[2048,1,512]{2,0,1:T(8,128)(2,1)} async-done(((bf16[256,1,512]{2,0,1:T(8,128)(2,1)}), bf16[2048,1,512]{2,0,1:T(8,128)(2,1)}) %all-gather.13.cloned.1.call-update) | async-done | bytes 2097168 | tf_op jit(solution)/shard_map/all_gather | solution.py:77
  227.2 38.5 %all_to_all.156 = bf16[4,2,90112]{2,1,0:T(2,128)(2,1)} all-to-all(bf16[4,2,90112]{2,1,0:T(2,128)(2,1)} %reshape.345), channel_id=1, replica_groups=mesh['fsdp'=8,'seq'=4] {'seq'}, dimensions={0} | all-to-all | bytes 2883584 | tf_op jit(solution)/shard_map/all_to_all | solution.py:72
  285.5 31.6 %reduce.1 = bf16[5632,64]{1,0:T(8,128)(2,1)S(1)} reduce(bf16[5632,1,64]{2,1,0:T(2,128)(2,1)} %bitcast.128, bf16[]{:T(256)} %broadcast.232), dimensions={1}, to_apply=%bitcast.94.reduce_sub_computation | reduce | bytes 1441794
  319.5 14.4 all_to_all.157
  343.9 94.4 %all-gather.17.cloned.1.call-done = bf16[2048,2,1408]{2,0,1:T(8,128)(2,1)} async-done(((bf16[256,2,1408]{2,0,1:T(8,128)(2,1)}), bf16[2048,2,1408]{2,0,1:T(8,128)(2,1)}) %all-gather.17.cloned.1.call-update) | async-done | bytes 11534352 | tf_op jit(solution)/shard_map/all_gather | solution.py:76
  438.4 15.4 copy.149
  461.2 12.6 fusion.58
  473.8 11.7 all-gather.21.cloned.1.call-done
  485.5 95.7 %all-gather.19.cloned.1.call-done = bf16[2048,1,1408]{2,0,1:T(8,128)(2,1)} async-done(((bf16[256,1,1408]{2,0,1:T(8,128)(2,1)}), bf16[2048,1,1408]{2,0,1:T(8,128)(2,1)}) %all-gather.19.cloned.1.call-update) | async-done | bytes 5767184 | tf_op jit(solution)/shard_map/all_gather | solution.py:77
  607.6 35.0 %reduce-scatter.11.cloned.1.call-done = f32[128,2048]{1,0:T(8,128)} async-done(((f32[512,2048]{1,0:T(8,128)}), f32[128,2048]{1,0:T(8,128)}) %reduce-scatter.11.cloned.1.call-update) | async-done | bytes 1048592 | tf_op jit(solution)/shard_map/reduce_scatter | solution.py:97
  644.2 45.3 %reduce-scatter.9.cloned.1.call-done = f32[128,2048]{1,0:T(8,128)} async-done(((f32[512,2048]{1,0:T(8,128)}), f32[128,2048]{1,0:T(8,128)}) %reduce-scatter.9.cloned.1.call-update) | async-done | bytes 1048592 | tf_op jit(solution)/shard_map/reduce_scatter | solution.py:97
  694.6 22.3 all-gather.23.cloned.1.call-done
  732.4 12.8 fusion.18
  745.2 26.9 %reshape.325 = f32[2048,2,1408]{2,1,0:T(2,128)} reshape(f32[2048,2816]{1,0:T(8,128)} %fusion.18) | data formatting | bytes 46137344 | tf_op jit(solution)/shard_map/reshape | solution.py:213
  796.3 18.1 copy.156
  828.2 178.0 %reduce-scatter.17.cloned.1.call-done = f32[256,1,1408]{0,2,1:T(8,128)} async-done(((f32[2048,1,1408]{0,2,1:T(8,128)}), f32[256,1,1408]{0,2,1:T(8,128)}) %reduce-scatter.17.cloned.1.call-update) | async-done | bytes 1441808 | tf_op jit(solution)/shard_map/reduce_scatter | solution.py:84
  1016.6 1175.3 %all-reduce.18.cloned.1.call-done = (f32[2048,3,512]{2,1,0:T(4,128)}, f32[2048,2,1408]{2,1,0:T(2,128)}) async-done(((f32[2048,3,512]{2,1,0:T(4,128)}, f32[2048,2,1408]{2,1,0:T(2,128)}), (f32[2048,3,512]{2,1,0:T(4,128)}, f32[2048,2,1408]{2,1,0:T(2,128)})) %all-reduce.18.cloned.1.call-update) | async-done | bytes 35651600
  2205.0 32.4 %all-to-all-done.4 = f32[256,3,512]{2,1,0:T(4,128)S(1)} async-done(((f32[256,3,512]{2,1,0:T(4,128)}), f32[256,3,512]{2,1,0:T(4,128)S(1)}, u32[]{:S(2)}, u32[]{:S(2)}) %all-to-all-start.4) | async-done | bytes 1572896 | tf_op jit(solution)/shard_map/all_to_all | solution.py:87
  2255.2 56.4 %all-reduce.13 = (f32[2048]{0:T(1024)S(1)}, f32[2048]{0:T(1024)S(1)}, f32[6144]{0:T(1024)S(1)}, f32[2048]{0:T(1024)S(1)}, f32[2048]{0:T(1024)S(1)}) all-reduce(f32[2048]{0:T(1024)S(1)} %get-tuple-element.14, f32[2048]{0:T(1024)S(1)} %get-tuple-element.17, ...), channel_id=6, replica_groups=mesh['fsdp'=8,'seq'=4] {'fsdp','seq'}, use_global_device_ids=true, to_apply=%region_16.17.clone | all-reduce | flops 14336 | bytes 114688
  (297 shorter events, 265.3 us)
Async XLA Ops:
  7.2 128.1 %all-gather.11.cloned.1.call-start = ((), (), s32[]{:S(2)}) async-start(), calls=%async_computation.15 | async-start | bytes 7077888 | tf_op jit(solution)/shard_map/all_gather | solution.py:76
  29.0 49.9 %copy-start.1 = (bf16[128,2048]{1,0:T(8,128)(2,1)S(1)}, bf16[128,2048]{1,0:T(8,128)(2,1)}, u32[]{:S(2)}) copy-start(bf16[128,2048]{1,0:T(8,128)(2,1)} %param.14) | copy-start | bytes 1572868
  32.0 49.2 %copy-start.35 = (bf16[64,2048]{1,0:T(8,128)(2,1)S(1)}, bf16[64,2048]{1,0:T(8,128)(2,1)}, u32[]{:S(2)}) copy-start(bf16[64,2048]{1,0:T(8,128)(2,1)} %param.21) | copy-start | bytes 786436
  34.2 124.0 %all-gather.9.cloned.1.call-start = ((), (), s32[]{:S(2)}) async-start(), calls=%async_computation.14 | async-start | bytes 2621440 | tf_op jit(solution)/shard_map/all_gather | solution.py:93
  95.1 9.6 all-to-all-start.1
  98.6 111.6 %all-gather.13.cloned.1.call-start = ((), (), s32[]{:S(2)}) async-start(), calls=%async_computation.16 | async-start | bytes 2359296 | tf_op jit(solution)/shard_map/all_gather | solution.py:77
  106.8 170.2 %reduce-scatter.7.cloned.1.call-start = ((), (), s32[]{:S(2)}) async-start(), calls=%async_computation.17 | async-start | bytes 5242880 | tf_op jit(solution)/shard_map/reduce_scatter | solution.py:97
  215.1 223.2 %all-gather.17.cloned.1.call-start = ((), (), s32[]{:S(2)}) async-start(), calls=%async_computation.19 | async-start | bytes 12976128 | tf_op jit(solution)/shard_map/all_gather | solution.py:76
  276.9 184.3 %all-gather.15.cloned.1.call-start = ((), (), s32[]{:S(2)}) async-start(), calls=%async_computation.18 | async-start | bytes 2621440 | tf_op jit(solution)/shard_map/all_gather | solution.py:93
  279.9 205.6 %all-gather.21.cloned.1.call-start = ((), (), s32[]{:S(2)}) async-start(), calls=%async_computation.22 | async-start | bytes 2621440 | tf_op jit(solution)/shard_map/all_gather | solution.py:93
  280.6 300.5 %all-gather.19.cloned.1.call-start = ((), (), s32[]{:S(2)}) async-start(), calls=%async_computation.20 | async-start | bytes 6488064 | tf_op jit(solution)/shard_map/all_gather | solution.py:77
  343.7 298.9 %reduce-scatter.11.cloned.1.call-start = ((), (), s32[]{:S(2)}) async-start(), calls=%async_computation.23 | async-start | bytes 5242880 | tf_op jit(solution)/shard_map/reduce_scatter | solution.py:97
  599.7 89.7 %reduce-scatter.9.cloned.1.call-start = ((), (), s32[]{:S(2)}) async-start(), calls=%async_computation.21 | async-start | bytes 5242880 | tf_op jit(solution)/shard_map/reduce_scatter | solution.py:97
  607.5 109.4 %all-gather.23.cloned.1.call-start = ((), (), s32[]{:S(2)}) async-start(), calls=%async_computation.24 | async-start | bytes 2621440 | tf_op jit(solution)/shard_map/all_gather | solution.py:93
  644.2 72.7 %copy-start.23 = (bf16[8,64,512]{2,1,0:T(8,128)(2,1)S(1)}, bf16[8,64,512]{2,1,0:T(8,128)(2,1)}, u32[]{:S(2)}) copy-start(bf16[8,64,512]{2,1,0:T(8,128)(2,1)} %copy-done.22) | copy-start | bytes 1572868
  694.2 128.2 %reduce-scatter.15.cloned.1.call-start = ((), (), s32[]{:S(2)}) async-start(), calls=%async_computation.26 | async-start | bytes 4718592 | tf_op jit(solution)/shard_map/reduce_scatter | solution.py:84
  721.8 284.4 %reduce-scatter.17.cloned.1.call-start = ((), (), s32[]{:S(2)}) async-start(), calls=%async_computation.27 | async-start | bytes 12976128 | tf_op jit(solution)/shard_map/reduce_scatter | solution.py:84
  730.8 1461.0 %all-reduce.18.cloned.1.call-start = ((), (), s32[]{:S(2)}) async-start(), calls=%async_computation.28 | async-start | bytes 79691776
  814.4 1437.5 %reduce-scatter.13.cloned.1.call-start = ((), (), s32[]{:S(2)}) async-start(), calls=%async_computation.25 | async-start | bytes 5242880 | tf_op jit(solution)/shard_map/reduce_scatter | solution.py:97
  824.7 186.3 %all-to-all-start.5 = ((f32[256,1,512]{2,1,0:T(1,128)}), f32[256,1,512]{2,1,0:T(1,128)S(1)}, u32[]{:S(2)}, u32[]{:S(2)}) async-start(f32[256,1,512]{2,1,0:T(1,128)} %copy.159), calls=%async_computation.10 | async-start | bytes 1048576 | tf_op jit(solution)/shard_map/all_to_all | solution.py:88
  828.2 187.1 %copy-start.59 = (u32[32]{0:T(128)S(1)}, u32[32]{0:T(128)}, u32[]{:S(2)}) copy-start(u32[32]{0:T(128)} %constant.71) | copy-start | bytes 388
  1011.7 1183.4 %all-to-all-start.7 = ((f32[256,1,1408]{2,1,0:T(1,128)}), f32[256,1,1408]{2,1,0:T(1,128)S(1)}, u32[]{:S(2)}, u32[]{:S(2)}) async-start(f32[256,1,1408]{2,1,0:T(1,128)} %copy.162), calls=%async_computation.13 | async-start | bytes 2883584 | tf_op jit(solution)/shard_map/all_to_all | solution.py:88
  2196.2 41.2 %all-to-all-start.4 = ((f32[256,3,512]{2,1,0:T(4,128)}), f32[256,3,512]{2,1,0:T(4,128)S(1)}, u32[]{:S(2)}, u32[]{:S(2)}) async-start(f32[256,3,512]{2,1,0:T(4,128)} %constant_dynamic-slice_fusion.1), calls=%async_computation.8 | async-start | bytes 4194304 | tf_op jit(solution)/shard_map/all_to_all | solution.py:87
  2238.8 88.6 %all-to-all-start.6 = ((f32[256,2,1408]{2,1,0:T(2,128)}), f32[256,2,1408]{2,1,0:T(2,128)S(1)}, u32[]{:S(2)}, u32[]{:S(2)}) async-start(f32[256,2,1408]{2,1,0:T(2,128)} %constant_dynamic-slice_fusion), calls=%async_computation.11 | async-start | bytes 5767168 | tf_op jit(solution)/shard_map/all_to_all | solution.py:87
  (61 other events, 563.1 us)
Sparse Core Ops, SparseCore 0:
  34.3 100.9 all-gather.10
  137.4 20.7 all-gather.8
  160.9 49.2 all-gather.12
  215.2 58.4 reduce-scatter.6
  277.1 161.2 all-gather.16
  440.4 20.7 all-gather.14
  462.8 22.5 all-gather.20
  488.5 92.6 all-gather.18
  599.9 42.6 reduce-scatter.10
  644.9 44.4 reduce-scatter.8
  694.3 22.5 all-gather.22
  721.9 87.9 reduce-scatter.14
  813.5 192.6 reduce-scatter.16
  1010.5 1181.3 all-reduce.17
  2194.2 57.5 reduce-scatter.12
where the time goes:
time: 2350 us; the launch traced here: 2340 us
  waiting for transfers between devices  1780 us (76%)
  local copies, waits for them, and re-layouts  180 us (8%)
  blocking collectives  168 us (7%)
  matrix products  106 us (5%)
  other arithmetic  69.2 us (3%)
    unnamed x16, waiting for transfers between devices  1180 us
    reduce_scatter x2, waiting for transfers between devices, return_block(): lax.psum_scatter(second, 'fsdp', scatter_dimension=0, tiled=True)  178 us
    all_gather x2, waiting for transfers between devices, fetch_block(): lax.all_gather(columns[1], 'fsdp', axis=0, tiled=True)  127 us
    all_gather x2, waiting for transfers between devices, fetch_block(): lax.all_gather(columns[0], 'fsdp', axis=0, tiled=True)  123 us
    unnamed x2, blocking collectives  99.8 us
    reduce_scatter x4, waiting for transfers between devices, seq_sums(): return lax.psum_scatter(values, 'seq', scatter_dimension=0, tiled=True)  87.9 us
    all_gather x4, waiting for transfers between devices, seq_rows(): return lax.all_gather(values, 'seq', axis=0, tiled=True)  55.4 us
    all_to_all x2, blocking collectives, fetch_block(): lax.all_to_all(first, 'seq', split_axis=2, concat_axis=0, tiled=True)  54.2 us
  transfers between devices with their start and end apart: 20, of which 15 were waited for; matrix products, arithmetic and copies ran while one was open for 12% of the time, Pallas kernels for 0%

commit v1 on v0

--- a/solution.py
+++ b/solution.py
@@ -5,6 +5,22 @@
 
 HEADS = 32
 HEAD_DIM = 64
+
+
+def ring_gather(x, axis, dim):
+    ways, here, step = (lax.axis_size(axis), lax.axis_index(axis), x.shape[dim])
+    shape = [n * ways if d == dim else n for d, n in enumerate(x.shape)]
+    full = lax.dynamic_update_slice_in_dim(jnp.zeros(shape, x.dtype), x, here * step, axis=dim)
+    going_up = going_down = x
+    for far in range(1, ways // 2 + 1):
+        going_up = lax.ppermute(going_up, axis, [(d, (d + 1) % ways) for d in range(ways)])
+        full = lax.dynamic_update_slice_in_dim(full, going_up, (here - far) % ways * step, axis=dim)
+        if 2 * far < ways:
+            going_down = lax.ppermute(going_down, axis, [(d, (d - 1) % ways) for d in range(ways)])
+            full = lax.dynamic_update_slice_in_dim(
+                full, going_down, (here + far) % ways * step, axis=dim
+            )
+    return full
 
 
 def layer_norm(values, gain, shift):
@@ -90,7 +106,7 @@
 
 
 def seq_rows(values):
-    return lax.all_gather(values, "seq", axis=0, tiled=True)
+    return ring_gather(values, "seq", 0)
 
 
 def seq_sums(values):

time: 2350 us -> 2280 us (0.970)
  waiting for transfers between devices: 1780 us -> 1690 us
    all_gather x4 -> x0, waiting for transfers between devices: 55.4 us -> none  [seq_rows(): return lax.all_gather(values, 'seq', axis=0, tiled=True)]
    all_gather x2, waiting for transfers between devices: 123 us -> 77.7 us  [fetch_block(): lax.all_gather(columns[0], 'fsdp', axis=0, tiled=True)]
    ppermute x0 -> x12, waiting for transfers between devices: none -> 43.7 us  [the longest x8 43.7 us: ring_gather(): lax.ppermute(going_up, axis, [(d, (d + 1) % ways) for d in range(ways)])]
    all_gather x2, waiting for transfers between devices: 127 us -> 87.4 us  [fetch_block(): lax.all_gather(columns[1], 'fsdp', axis=0, tiled=True)]
    unnamed x16 -> x12, waiting for transfers between devices: 1180 us -> 1180 us
    unnamed x161 -> x162, local copies, waits for them, and re-layouts: 47.5 us -> 47.6 us
  transfers between devices with their start and end apart: 20 -> 28, of which waited for: 15 -> 17; matrix products, arithmetic and copies ran while one was open for 12% -> 13% of each run, Pallas kernels for 0% -> 0%
where the time goes in v1:
time: 2280 us; the launch traced here: 2270 us
  waiting for transfers between devices  1690 us (74%)
  local copies, waits for them, and re-layouts  196 us (9%)
  blocking collectives  168 us (7%)
  matrix products  106 us (5%)
  other arithmetic  67.7 us (3%)
  starting transfers between devices  27.3 us (1%)
    unnamed x12, waiting for transfers between devices  1180 us
    reduce_scatter x2, waiting for transfers between devices, return_block(): lax.psum_scatter(second, 'fsdp', scatter_dimension=0, tiled=True)  178 us
    unnamed x2, blocking collectives  99.8 us
    all_gather x2, waiting for transfers between devices, fetch_block(): lax.all_gather(columns[1], 'fsdp', axis=0, tiled=True)  87.4 us
    reduce_scatter x4, waiting for transfers between devices, seq_sums(): return lax.psum_scatter(values, 'seq', scatter_dimension=0, tiled=True)  87.2 us
    all_gather x2, waiting for transfers between devices, fetch_block(): lax.all_gather(columns[0], 'fsdp', axis=0, tiled=True)  77.7 us
    all_to_all x2, blocking collectives, fetch_block(): lax.all_to_all(first, 'seq', split_axis=2, concat_axis=0, tiled=True)  54.2 us
    unnamed x162, local copies, waits for them, and re-layouts  47.6 us
  transfers between devices with their start and end apart: 28, of which 17 were waited for; matrix products, arithmetic and copies ran while one was open for 13% of the time, Pallas kernels for 0%

profile of v1, /device:TPU:0, one launch (start us, length us, event | category | flops | bytes accessed | tf_op | source)
XLA Modules:
  0.0 2266.7 jit_solution(17646020488042857118)
XLA Ops:
  13.2 15.8 all_to_all.155
  35.5 43.4 %all-reduce.15 = (bf16[2048]{0:T(1024)(128)(2,1)S(1)}, bf16[2048]{0:T(1024)(128)(2,1)S(1)}, bf16[3,2048]{1,0:T(4,128)(2,1)S(1)}, bf16[2048]{0:T(1024)(128)(2,1)}, bf16[2048]{0:T(1024)(128)(2,1)}) all-reduce(bf16[2048]{0:T(1024)(128)(2,1)S(1)} %dynamic-update-slice.1, ...), channel_id=1, replica_groups=mesh['fsdp'=8,'seq'=4] {'fsdp','seq'}, use_global_device_ids=true, to_apply=%add.1 | all-reduce | flops 14336 | bytes 57344
  83.2 11.5 reduce
  113.0 22.2 all-gather.5.cloned.1.call-done
  163.9 21.7 all-gather.7.cloned.1.call-done
  202.5 38.4 %all_to_all.156 = bf16[4,2,90112]{2,1,0:T(2,128)(2,1)} all-to-all(bf16[4,2,90112]{2,1,0:T(2,128)(2,1)} %reshape.345), channel_id=1, replica_groups=mesh['fsdp'=8,'seq'=4] {'seq'}, dimensions={0} | all-to-all | bytes 2883584 | tf_op jit(solution)/shard_map/all_to_all | solution.py:88
  258.5 31.7 %reduce.1 = bf16[5632,64]{1,0:T(8,128)(2,1)} reduce(bf16[5632,1,64]{2,1,0:T(2,128)(2,1)S(1)} %bitcast.126, bf16[]{:T(256)} %broadcast.239), dimensions={1}, to_apply=%bitcast.92.reduce_sub_computation | reduce | bytes 1441794
  293.2 14.1 all_to_all.157
  319.3 12.0 collective-permute-done.6
  358.2 55.5 %all-gather.9.cloned.1.call-done = bf16[2048,2,1408]{2,0,1:T(8,128)(2,1)} async-done(((bf16[256,2,1408]{2,0,1:T(8,128)(2,1)}), bf16[2048,2,1408]{2,0,1:T(8,128)(2,1)}) %all-gather.9.cloned.1.call-update) | async-done | bytes 11534352 | tf_op jit(solution)/shard_map/all_gather | solution.py:92
  413.7 15.3 copy.148
  428.9 12.7 fusion.61
  441.6 65.8 %all-gather.11.cloned.1.call-done = bf16[2048,1,1408]{2,0,1:T(8,128)(2,1)} async-done(((bf16[256,1,1408]{2,0,1:T(8,128)(2,1)}), bf16[2048,1,1408]{2,0,1:T(8,128)(2,1)}) %all-gather.11.cloned.1.call-update) | async-done | bytes 5767184 | tf_op jit(solution)/shard_map/all_gather | solution.py:93
  507.4 10.5 fusion.12
  535.8 34.1 %reduce-scatter.11.cloned.1.call-done = f32[128,2048]{1,0:T(8,128)} async-done(((f32[512,2048]{1,0:T(8,128)}), f32[128,2048]{1,0:T(8,128)}) %reduce-scatter.11.cloned.1.call-update) | async-done | bytes 1048592 | tf_op jit(solution)/shard_map/reduce_scatter | solution.py:113
  571.5 45.4 %reduce-scatter.9.cloned.1.call-done = f32[128,2048]{1,0:T(8,128)} async-done(((f32[512,2048]{1,0:T(8,128)}), f32[128,2048]{1,0:T(8,128)}) %reduce-scatter.9.cloned.1.call-update) | async-done | bytes 1048592 | tf_op jit(solution)/shard_map/reduce_scatter | solution.py:113
  622.3 11.0 collective-permute-done.9
  657.2 12.7 fusion.18
  669.9 26.9 %reshape.325 = f32[2048,2,1408]{2,1,0:T(2,128)} reshape(f32[2048,2816]{1,0:T(8,128)} %fusion.18) | data formatting | bytes 46137344 | tf_op jit(solution)/shard_map/reshape | solution.py:229
  721.0 18.1 copy.155
  752.9 177.6 %reduce-scatter.17.cloned.1.call-done = f32[256,1,1408]{2,0,1:T(8,128)} async-done(((f32[2048,1,1408]{2,0,1:T(8,128)}), f32[256,1,1408]{2,0,1:T(8,128)}) %reduce-scatter.17.cloned.1.call-update) | async-done | bytes 1441808 | tf_op jit(solution)/shard_map/reduce_scatter | solution.py:100
  940.1 1176.1 %all-reduce.18.cloned.1.call-done = (f32[2048,3,512]{2,1,0:T(4,128)}, f32[2048,2,1408]{2,1,0:T(2,128)}) async-done(((f32[2048,3,512]{2,1,0:T(4,128)}, f32[2048,2,1408]{2,1,0:T(2,128)}), (f32[2048,3,512]{2,1,0:T(4,128)}, f32[2048,2,1408]{2,1,0:T(2,128)})) %all-reduce.18.cloned.1.call-update) | async-done | bytes 35651600
  2129.3 32.4 %all-to-all-done.4 = f32[256,3,512]{2,1,0:T(4,128)S(1)} async-done(((f32[256,3,512]{2,1,0:T(4,128)}), f32[256,3,512]{2,1,0:T(4,128)S(1)}, u32[]{:S(2)}, u32[]{:S(2)}) %all-to-all-start.4) | async-done | bytes 1572896 | tf_op jit(solution)/shard_map/all_to_all | solution.py:103
  2179.6 56.4 %all-reduce.13 = (f32[2048]{0:T(1024)S(1)}, f32[2048]{0:T(1024)S(1)}, f32[6144]{0:T(1024)S(1)}, f32[2048]{0:T(1024)S(1)}, f32[2048]{0:T(1024)S(1)}) all-reduce(f32[2048]{0:T(1024)S(1)} %get-tuple-element.14, f32[2048]{0:T(1024)S(1)} %get-tuple-element.17, ...), channel_id=6, replica_groups=mesh['fsdp'=8,'seq'=4] {'fsdp','seq'}, use_global_device_ids=true, to_apply=%region_16.17.clone | all-reduce | flops 14336 | bytes 114688
  (327 shorter events, 289.6 us)
Async XLA Ops:
  7.2 128.0 %all-gather.5.cloned.1.call-start = ((), (), s32[]{:S(2)}) async-start(), calls=%async_computation.14 | async-start | bytes 7077888 | tf_op jit(solution)/shard_map/all_gather | solution.py:92
  80.1 21.5 collective-permute-start
  80.1 28.9 %collective-permute-start.1 = (bf16[128,2048]{1,0:T(8,128)(2,1)S(1)}, bf16[128,2048]{1,0:T(8,128)(2,1)}, u32[]{:S(2)}, u32[]{:S(2)}) collective-permute-start(bf16[128,2048]{1,0:T(8,128)(2,1)S(1)} %get-tuple-element.40), channel_id=1, source_target_pairs={{0,3},{1,0},{2,1},{3,2},{4,7},{5,4},{6,5},{7,6},{8,11},{9,8},{10,9... | collective-permute-start | bytes 1572872 | tf_op jit(solution)/shard_map/ppermute | solution.py:19
  99.4 86.2 %all-gather.7.cloned.1.call-start = ((), (), s32[]{:S(2)}) async-start(), calls=%async_computation.15 | async-start | bytes 2359296 | tf_op jit(solution)/shard_map/all_gather | solution.py:93
  108.2 223.2 %reduce-scatter.7.cloned.1.call-start = ((), (), s32[]{:S(2)}) async-start(), calls=%async_computation.16 | async-start | bytes 5242880 | tf_op jit(solution)/shard_map/reduce_scatter | solution.py:113
  190.5 223.2 %all-gather.9.cloned.1.call-start = ((), (), s32[]{:S(2)}) async-start(), calls=%async_computation.17 | async-start | bytes 12976128 | tf_op jit(solution)/shard_map/all_gather | solution.py:92
  252.2 255.1 %all-gather.11.cloned.1.call-start = ((), (), s32[]{:S(2)}) async-start(), calls=%async_computation.18 | async-start | bytes 6488064 | tf_op jit(solution)/shard_map/all_gather | solution.py:93
  317.5 252.4 %reduce-scatter.11.cloned.1.call-start = ((), (), s32[]{:S(2)}) async-start(), calls=%async_computation.20 | async-start | bytes 5242880 | tf_op jit(solution)/shard_map/reduce_scatter | solution.py:113
  317.5 13.9 collective-permute-start.6
  317.6 23.1 %collective-permute-start.7 = (bf16[128,2048]{1,0:T(8,128)(2,1)S(1)}, bf16[128,2048]{1,0:T(8,128)(2,1)}, u32[]{:S(2)}, u32[]{:S(2)}) collective-permute-start(bf16[128,2048]{1,0:T(8,128)(2,1)S(1)} %copy-done.9), channel_id=1, source_target_pairs={{0,3},{1,0},{2,1},{3,2},{4,7},{5,4},{6,5},{7,6},{8,11},{9,8},{10,9... | collective-permute-start | bytes 1572872 | tf_op jit(solution)/shard_map/ppermute | solution.py:19
  331.4 17.3 collective-permute-start.8
  335.8 12.8 collective-permute-start.3
  339.0 11.4 collective-permute-start.4
  527.0 89.9 %reduce-scatter.9.cloned.1.call-start = ((), (), s32[]{:S(2)}) async-start(), calls=%async_computation.19 | async-start | bytes 5242880 | tf_op jit(solution)/shard_map/reduce_scatter | solution.py:113
  535.7 211.3 %reduce-scatter.15.cloned.1.call-start = ((), (), s32[]{:S(2)}) async-start(), calls=%async_computation.22 | async-start | bytes 4718592 | tf_op jit(solution)/shard_map/reduce_scatter | solution.py:100
  620.1 13.2 collective-permute-start.9
  620.2 13.2 collective-permute-start.10
  646.7 283.9 %reduce-scatter.17.cloned.1.call-start = ((), (), s32[]{:S(2)}) async-start(), calls=%async_computation.23 | async-start | bytes 12976128 | tf_op jit(solution)/shard_map/reduce_scatter | solution.py:100
  655.9 1460.3 %all-reduce.18.cloned.1.call-start = ((), (), s32[]{:S(2)}) async-start(), calls=%async_computation.24 | async-start | bytes 79691776
  739.1 1437.1 %reduce-scatter.13.cloned.1.call-start = ((), (), s32[]{:S(2)}) async-start(), calls=%async_computation.21 | async-start | bytes 5242880 | tf_op jit(solution)/shard_map/reduce_scatter | solution.py:113
  749.4 185.1 %all-to-all-start.5 = ((f32[256,1,512]{2,1,0:T(1,128)}), f32[256,1,512]{2,1,0:T(1,128)S(1)}, u32[]{:S(2)}, u32[]{:S(2)}) async-start(f32[256,1,512]{2,1,0:T(1,128)} %copy.158), calls=%async_computation.10 | async-start | bytes 1048576 | tf_op jit(solution)/shard_map/all_to_all | solution.py:104
  935.3 1184.2 %all-to-all-start.7 = ((f32[256,1,1408]{2,1,0:T(1,128)}), f32[256,1,1408]{2,1,0:T(1,128)S(1)}, u32[]{:S(2)}, u32[]{:S(2)}) async-start(f32[256,1,1408]{2,1,0:T(1,128)} %copy.161), calls=%async_computation.13 | async-start | bytes 2883584 | tf_op jit(solution)/shard_map/all_to_all | solution.py:104
  2120.6 41.2 %all-to-all-start.4 = ((f32[256,3,512]{2,1,0:T(4,128)}), f32[256,3,512]{2,1,0:T(4,128)S(1)}, u32[]{:S(2)}, u32[]{:S(2)}) async-start(f32[256,3,512]{2,1,0:T(4,128)} %constant_dynamic-slice_fusion.2), calls=%async_computation.8 | async-start | bytes 4194304 | tf_op jit(solution)/shard_map/all_to_all | solution.py:103
  2163.1 88.5 %all-to-all-start.6 = ((f32[256,2,1408]{2,1,0:T(2,128)}), f32[256,2,1408]{2,1,0:T(2,128)S(1)}, u32[]{:S(2)}, u32[]{:S(2)}) async-start(f32[256,2,1408]{2,1,0:T(2,128)} %constant_dynamic-slice_fusion.1), calls=%async_computation.11 | async-start | bytes 5767168 | tf_op jit(solution)/shard_map/all_to_all | solution.py:103
  (70 other events, 945.2 us)
Sparse Core Ops, SparseCore 0:
  34.3 100.8 all-gather.4
  137.9 47.6 all-gather.6
  190.6 58.4 reduce-scatter.6
  252.4 161.2 all-gather.8
  416.5 90.8 all-gather.10
  527.2 42.6 reduce-scatter.10
  572.4 44.4 reduce-scatter.8
  646.8 87.6 reduce-scatter.14
  738.1 192.4 reduce-scatter.16
  934.9 1181.2 all-reduce.17
  2118.7 57.4 reduce-scatter.12
